TPU v7x, 128 devices: a whole 4x4x4 slice. The times are simulated.
128 devices in a mesh: db: 64 (over z, y, x), mp: 2 (over core).
Axes of the slice: x: 4, y: 4, z: 4, core: 2. Of those that a mesh axis runs over, the one named last changes fastest.
Arguments:
- queries: bfloat16 [57344, 4096], P('db', 'mp'), may hold values from -600 to 600
- database: bfloat16 [2048, 128, 896], P('db', 'mp'), may hold values from -300 to 300
- neighbour_shard: int32 [896, 2], P('db'), may hold values from 0 to 63, all different within a row; in each aligned block of 14 rows (0 to 13, 14 to 27, ...) at most 2 rows name the same one
- neighbour_row: int32 [896, 2], P('db'), may hold values from 0 to 31
- w_key: bfloat16 [896, 4096], P(None, 'mp'), may hold values from -0.1875 to 0.1875
- w_value: bfloat16 [896, 4096], P(None, 'mp'), may hold values from -0.1875 to 0.1875
Outputs:
- attended: bfloat16 [57344, 4096], P('db', 'mp')
Inputs may be any that keep to these rules, and one draw needn't show every extreme that they name: `neighbour_shard`: within the spans of one index of db no shard is named more than 2 times, and in every draw some shard is named exactly 2 times by some index; the 2 neighbours of a span lie in different shards.
All inputs are finite; a program needn't handle non-finite values.
Results may differ from a plain program's by a relative error of at most 0.01.
The roundings to bfloat16 on the way count: a program that leaves them out, or rounds other values in their place, can miss the bound.
Values may be sent and summed in bfloat16 or wider, within the bound.
A program may use at most 192 MiB of HBM per device.

v0:
```python
import math

import jax
import jax.numpy as jnp
from jax import lax
from jax.sharding import PartitionSpec as P

HD = 128
E = 896
CAP = 2


def rank_in_shard(shard_list):
    positions = jnp.arange(shard_list.shape[0])
    earlier = (shard_list[:, None] == shard_list[None, :]) & (
        positions[None, :] < positions[:, None]
    )
    return jnp.sum(earlier.astype(jnp.int32), axis=1)


def requests_for(shard_list, slot_list, row_list, shard_ids):
    matched = (shard_list[:, None, None] == shard_ids[None, :, None]) & (
        slot_list[:, None, None] == jnp.arange(CAP)[None, None, :]
    )
    return jnp.sum(matched.astype(jnp.int32) * row_list[:, None, None], axis=0)


def attend(fetched, queries, w_key, w_value, span_total):
    squares = jnp.einsum("pre,pre->pr", fetched, fetched, preferred_element_type=jnp.float32)
    inverse = lax.rsqrt(squares / E + 1e-06)
    encoded = (fetched.astype(jnp.float32) * inverse[..., None]).astype(jnp.bfloat16)
    encoded_rows = encoded.reshape(-1, E)
    key_rows = jnp.dot(encoded_rows, w_key, preferred_element_type=jnp.float32).astype(jnp.bfloat16)
    value_rows = jnp.dot(encoded_rows, w_value, preferred_element_type=jnp.float32).astype(
        jnp.bfloat16
    )
    local_width = w_key.shape[1]
    head_local = local_width // HD
    span_rows = queries.shape[0] // span_total
    key_rows = key_rows.reshape(span_total, -1, head_local, HD)
    value_rows = value_rows.reshape(span_total, -1, head_local, HD)
    grouped = queries.reshape(span_total, span_rows, head_local, HD)
    scores = jnp.einsum("cmhd,cnhd->chmn", grouped, key_rows, preferred_element_type=jnp.float32)
    scores = scores * (1.0 / math.sqrt(HD))
    weights = jax.nn.softmax(scores, axis=-1).astype(jnp.bfloat16)
    attended = jnp.einsum(
        "chmn,cnhd->cmhd", weights, value_rows, preferred_element_type=jnp.float32
    )
    return attended.astype(jnp.bfloat16).reshape(queries.shape[0], local_width)


def body(queries, database, neighbour_shard, neighbour_row, w_key, w_value):
    shards = lax.axis_size("db")
    core_total = lax.axis_size("mp")
    span_total = neighbour_shard.shape[0]
    request_total = span_total * neighbour_shard.shape[1]
    shard_list = neighbour_shard.reshape(request_total)
    row_list = neighbour_row.reshape(request_total)
    slot_list = rank_in_shard(shard_list)
    wanted = requests_for(shard_list, slot_list, row_list, jnp.arange(shards))
    asked = lax.all_to_all(wanted, "db", split_axis=0, concat_axis=0, tiled=True)
    outgoing = database[asked]
    half_rows = database.shape[1]
    doubled = jnp.broadcast_to(outgoing[:, None], (shards, core_total, CAP, half_rows, E))
    doubled = doubled.reshape(shards * core_total, CAP, half_rows, E)
    arrived = lax.all_to_all(doubled, ("db", "mp"), split_axis=0, concat_axis=0, tiled=True)
    arrived = arrived.reshape(shards, core_total, CAP, half_rows, E)
    picked = arrived[shard_list, :, slot_list]
    fetched = picked.reshape(request_total, core_total * half_rows, E)
    return attend(fetched, queries, w_key, w_value, span_total)


def solution(mesh):
    placed = (
        P("db", "mp"),
        P("db", "mp", None),
        P("db", None),
        P("db", None),
        P(None, "mp"),
        P(None, "mp"),
    )
    return jax.shard_map(body, mesh=mesh, in_specs=placed, out_specs=P("db", "mp"), check_vma=False)
```

profile of v0, /device:TPU:28, one launch (start us, length us, event | category | flops | bytes accessed | tf_op | source)
XLA Modules:
  0.0 671.1 jit_solution(10537156505853182014)
XLA Ops:
  0.0 0.8 copy.32
  0.8 0.1 eq.51
  0.9 0.2 convert_reduce_fusion
  1.0 0.1 iota_compare_fusion.2
  1.1 0.1 iota_compare_fusion
  1.2 0.8 copy.33
  2.0 0.1 mul.30
  2.0 0.1 fusion.23
  2.2 0.1 copy.34
  2.3 17.0 %all_to_all.17 = s32[64,1,2]{2,1,0:T(1,128)S(1)} all-to-all(s32[64,1,2]{2,1,0:T(1,128)S(1)} %copy.34), channel_id=1, replica_groups=mesh['db'=64,'mp'=2] {'db'}, dimensions={0} | all-to-all | bytes 1024 | tf_op jit(solution)/shard_map/all_to_all | solution.py:61
  19.3 0.1 copy.35
  19.4 0.1 copy.36
  19.5 0.1 reshape.168
  19.7 11.0 %gather_fusion = bf16[128,64,896]{2,1,0:T(8,128)(2,1)} fusion(bf16[32,64,896]{2,1,0:T(8,128)(2,1)} %param.7, s32[1024]{0:T(1024)S(1)} %pad_clamp_fusion), kind=kCustom, calls=%fused_computation | custom fusion | bytes 29360640 | tf_op jit(solution)/shard_map/gather | solution.py:62
  30.7 14.2 %broadcast_in_dim.2 = bf16[64,2,2,64,896]{4,3,2,1,0:T(8,128)(2,1)} broadcast(bf16[64,2,64,896]{3,2,1,0:T(8,128)(2,1)} %bitcast.64), dimensions={0,2,3,4} | broadcast | bytes 44040192 | tf_op jit(solution)/shard_map/broadcast_in_dim | solution.py:64
  44.9 9.4 %all-to-all-start.1 = ((bf16[128,2,64,896]{3,2,1,0:T(8,128)(2,1)}), bf16[128,2,64,896]{3,2,1,0:T(8,128)(2,1)}, u32[]{:S(2)}, u32[]{:S(2)}) async-start(bf16[128,2,64,896]{3,2,1,0:T(8,128)(2,1)} %bitcast.62), calls=%async_computation.1 | async-start | bytes 58720256 | tf_op jit(solution)/shard_map/all_to_all | solution.py:66
  54.2 0.1 reshape.159
  54.3 5.1 copy.47
  59.4 469.4 %all-to-all-done.1 = bf16[128,2,64,896]{3,2,1,0:T(8,128)(2,1)} async-done(((bf16[128,2,64,896]{3,2,1,0:T(8,128)(2,1)}), bf16[128,2,64,896]{3,2,1,0:T(8,128)(2,1)}, u32[]{:S(2)}, u32[]{:S(2)}) %all-to-all-start.1) | async-done | bytes 29360160 | tf_op jit(solution)/shard_map/all_to_all | solution.py:66
  528.8 13.4 %gather_fusion.1 = bf16[28,2,64,896]{3,2,1,0:T(8,128)(2,1)} fusion(bf16[64,2,2,64,896]{4,3,2,1,0:T(8,128)(2,1)} %bitcast.4, s32[28]{0:T(128)S(1)} %fusion.31), kind=kCustom, calls=%fused_computation.1 | custom fusion | bytes 12845280 | tf_op jit(solution)/shard_map/gather | solution.py:68
  542.2 0.0 copy-start.3
  542.2 4.3 fusion.11
  546.5 4.0 fusion.10
  550.5 0.0 copy-done.3
  550.5 0.0 copy-start.1
  550.5 16.0 %fusion.13 = bf16[448,8,16,128]{3,1,2,0:T(8,128)(2,1)S(1)} fusion(bf16[3584,896]{1,0:T(8,128)(2,1)S(1)} %fusion.10, bf16[896,2048]{1,0:T(8,128)(2,1)S(1)} %copy-done.3), kind=kOutput, calls=%fused_computation.20 | convolution fusion | flops 13160677376 | bytes 24772608 | tf_op jit(solution)/shard_map/dot_general | solution.py:33
  566.4 0.0 copy-done.1
  566.4 0.0 copy-start
  566.5 7.6 %copy.46 = bf16[448,8,16,128]{3,2,1,0:T(8,128)(2,1)} copy(bf16[448,8,16,128]{3,1,2,0:T(8,128)(2,1)S(1)} %fusion.13) | data formatting | bytes 29360128
  574.1 0.0 copy-done
  574.1 13.4 %fusion.5 = f32[14,16,256,64]{2,3,1,0:T(8,128)} fusion(bf16[14,256,16,128]{3,2,1,0:T(8,128)(2,1)} %bitcast.63, bf16[14,64,16,128]{3,2,1,0:T(8,128)(2,1)S(1)} %bitcast.65), kind=kOutput, calls=%fused_computation.11 | convolution fusion | flops 939524096 | bytes 33030144 | tf_op jit(solution)/shard_map/cmhd,cnhd->chmn/dot_general | solution.py:43
  587.5 0.0 copy-start.2
  587.5 0.0 copy-start.4
  587.5 15.1 %fusion.35 = f32[14,16,64]{2,1,0:T(8,128)S(1)} fusion(f32[14,16,256,64]{2,3,1,0:T(8,128)} %fusion.5), kind=kOutput, calls=%fused_computation.47 | output fusion | flops 14680319 | bytes 14737408 | tf_op jit(solution)/shard_map/sub | solution.py:45
  602.6 0.0 copy-done.2
  602.6 0.0 copy-done.4
  602.6 16.0 %fusion.12 = bf16[448,8,16,128]{3,1,2,0:T(8,128)(2,1)S(1)} fusion(bf16[3584,896]{1,0:T(8,128)(2,1)S(1)} %copy-done.2, bf16[896,2048]{1,0:T(8,128)(2,1)S(1)} %copy-done.4), kind=kOutput, calls=%fused_computation.19 | convolution fusion | flops 13160677376 | bytes 24772608 | tf_op jit(solution)/shard_map/dot_general | solution.py:34
  618.6 7.6 %copy.48 = bf16[448,8,16,128]{3,2,1,0:T(8,128)(2,1)} copy(bf16[448,8,16,128]{3,1,2,0:T(8,128)(2,1)S(1)} %fusion.12) | data formatting | bytes 29360128
  626.2 36.0 %convert_bitcast_fusion = bf16[14,64,16,128]{3,1,2,0:T(8,128)(2,1)} fusion(bf16[14,256,16,128]{3,2,1,0:T(8,128)(2,1)} %bitcast.66, f32[14,16,64]{2,1,0:T(8,128)S(1)} %fusion.35, f32[14,16,256,64]{2,3,1,0:T(8,128)} %fusion.5), kind=kOutput, calls=%fused_computation.25 | convolution fusion | flops 959723776 | bytes 33087488 | tf_op jit(solution)/shard_map/chmn,cnhd->cmhd/dot_general | solution.py:46
  662.2 5.0 copy.41
  667.2 3.7 copy.59
  (4 shorter events, 0.0 us)
Async XLA Ops:
  44.9 483.9 %all-to-all-start.1 = ((bf16[128,2,64,896]{3,2,1,0:T(8,128)(2,1)}), bf16[128,2,64,896]{3,2,1,0:T(8,128)(2,1)}, u32[]{:S(2)}, u32[]{:S(2)}) async-start(bf16[128,2,64,896]{3,2,1,0:T(8,128)(2,1)} %bitcast.62), calls=%async_computation.1 | async-start | bytes 58720256 | tf_op jit(solution)/shard_map/all_to_all | solution.py:66
  542.2 8.3 %copy-start.3 = (bf16[896,2048]{1,0:T(8,128)(2,1)S(1)}, bf16[896,2048]{1,0:T(8,128)(2,1)}, u32[]{:S(2)}) copy-start(bf16[896,2048]{1,0:T(8,128)(2,1)} %param.10) | copy-start | bytes 11010052
  550.5 16.0 %copy-start.1 = (bf16[3584,896]{1,0:T(8,128)(2,1)}, bf16[3584,896]{1,0:T(8,128)(2,1)S(1)}, u32[]{:S(2)}) copy-start(bf16[3584,896]{1,0:T(8,128)(2,1)S(1)} %fusion.10) | copy-start | bytes 19267588
  566.4 7.6 %copy-start = (bf16[112,8,16,128]{3,2,1,0:T(8,128)(2,1)S(1)}, bf16[112,8,16,128]{3,2,1,0:T(8,128)(2,1)}, u32[]{:S(2)}) copy-start(bf16[112,8,16,128]{3,2,1,0:T(8,128)(2,1)} %copy.47) | copy-start | bytes 11010052
  587.5 15.1 %copy-start.2 = (bf16[3584,896]{1,0:T(8,128)(2,1)S(1)}, bf16[3584,896]{1,0:T(8,128)(2,1)}, u32[]{:S(2)}) copy-start(bf16[3584,896]{1,0:T(8,128)(2,1)} %copy-done.1) | copy-start | bytes 19267588
  587.5 15.1 %copy-start.4 = (bf16[896,2048]{1,0:T(8,128)(2,1)S(1)}, bf16[896,2048]{1,0:T(8,128)(2,1)}, u32[]{:S(2)}) copy-start(bf16[896,2048]{1,0:T(8,128)(2,1)} %param.11) | copy-start | bytes 11010052
where the time goes:
time: 675 us; the launch traced here: 671 us
  waiting for transfers between devices  469 us (69%)
  matrix products  81.3 us (12%)
  local copies, waits for them, and re-layouts  69.8 us (10%)
  other arithmetic  23.8 us (4%)
  blocking collectives  17 us (3%)
  starting transfers between devices  9.36 us (1%)
    all_to_all x1, waiting for transfers between devices, body(): lax.all_to_all(doubled, ('db', 'mp'), split_axis=0, concat_axis=0, tiled=...  469 us
    dot_general x1, matrix products, attend(): jnp.einsum('chmn,cnhd->cmhd', weights, value_rows, preferred_element_type...  36 us
    unnamed x16, local copies, waits for them, and re-layouts  25.5 us
    all_to_all x1, blocking collectives, body(): lax.all_to_all(wanted, 'db', split_axis=0, concat_axis=0, tiled=True)  17 us
    dot_general x1, matrix products, attend(): jnp.dot(encoded_rows, w_key, preferred_element_type=jnp.float32)  16 us
    dot_general x1, matrix products, attend(): jnp.dot(encoded_rows, w_value, preferred_element_type=jnp.float32)  16 us
    sub x1, other arithmetic, attend(): weights = jax.nn.softmax(scores, axis=-1).astype(jnp.bfloat16)  15.1 us
    broadcast_in_dim x1, local copies, waits for them, and re-layouts, body(): jnp.broadcast_to(outgoing[:, None], (shards, core_total, CAP, half_rows, E))  14.2 us
  transfers between devices with their start and end apart: 1, of which 1 were waited for; matrix products, arithmetic and copies ran while one was open for 1% of the time, Pallas kernels for 0%

commit v1 on v0

v1 whole, which is shorter than its diff:
```python
import functools
import math

import jax
import jax.numpy as jnp
from jax import lax
from jax.experimental import pallas as pl
from jax.experimental.pallas import tpu as pltpu
from jax.sharding import PartitionSpec as P

MESH = pl.DeviceIdType.MESH
HD = 128
E = 896
STRIDES = (16, 4, 1)
PARTS = ((0, 256), (256, 256), (512, 384))
VARIANTS = ((24, 16, 13), (25, 20, 14), (26, 24, 16), (32, 32, 28))

SHIFTS = (4, 2, 0)
LANES = 128
RMAX = 32
f32 = jnp.float32


def iota(shape, axis):
    return lax.broadcasted_iota(jnp.int32, shape, axis)


def with_coord(n, shift, value):
    return n - (((n >> shift) & 3) << shift) + (value << shift)


def mm(a, b):
    return jnp.dot(a.astype(jnp.bfloat16), b.astype(jnp.bfloat16), preferred_element_type=f32)


def route_kernel(me_ref, g_ref, out_ref, present):
    me = me_ref[0]
    every = g_ref[...]
    named = jnp.concatenate(
        [jnp.max(every[4 * i : 4 * i + 4], axis=0, keepdims=True) for i in range(16)], axis=1
    )
    lane = iota((LANES, LANES), 1)
    sub = iota((LANES, LANES), 0)
    strict = (lane < sub).astype(f32)
    strict_block = jnp.where((lane < sub) & ((lane >> 5) == (sub >> 5)), 1.0, 0.0)
    upper = (sub < lane).astype(f32)

    def members(i):
        z, y, x = i // 4, i % 4, sub >> 5
        own = (jnp.full_like(x, z), jnp.full_like(x, y), x)
        inside = jnp.zeros((LANES, LANES), jnp.bool_)
        for p in range(3):
            a, b = own[p], own[(p + 1) % 3]
            inside = inside | ((lane >> 2 == p) & ((lane & 3) == a))
            inside = inside | ((lane >> 4 == p + 1) & ((lane & 15) == a * 4 + b))
        return inside.astype(jnp.bfloat16)

    group = jnp.concatenate([members(i) for i in range(16)], axis=0)
    totals = []
    for block in range(16):
        code = iota((LANES, 2048), 0) + block * LANES
        hit = (code == named).astype(jnp.bfloat16)
        there = (jnp.dot(hit, group, preferred_element_type=f32) > 0.5).astype(f32)
        present[block * LANES : (block + 1) * LANES, :] = there
        totals.append(jnp.concatenate(
            [jnp.sum(there[32 * q : 32 * q + 32], axis=0, keepdims=True) for q in range(4)], axis=0))
    total = jnp.concatenate(totals, axis=0)
    lane64 = iota((64, LANES), 1)
    need1 = jnp.max(jnp.where(lane64 < 12, total, 0.0))
    shard = iota((16, 64), 1)
    key = iota((16, 64), 0)
    need2 = jnp.zeros((), f32)
    need3 = jnp.zeros((), f32)
    valid_all = every >= 0
    for p in range(3):
        a, b, c = SHIFTS[p], SHIFTS[(p + 1) % 3], SHIFTS[(p + 2) % 3]
        pick = (((shard >> b) & 3) * 4 + ((shard >> c) & 3) == key).astype(f32)
        line = mm(pick, total)
        lane16 = iota((16, LANES), 1)
        need2 = jnp.maximum(need2, jnp.max(jnp.where(lane16 >> 4 == p + 1, line, 0.0)))
        for v in range(4):
            here = valid_all & (((every >> (5 + c)) & 3) == v)
            need3 = jnp.maximum(need3, jnp.max(jnp.sum(here.astype(f32), axis=1, keepdims=True)))

    rows1 = iota((32, LANES), 0)
    mine = present[pl.ds(pl.multiple_of(me * 32, 32), 32), :]
    rank0 = mm(strict[:32, :32], mine)
    table = []
    for j in range(RMAX):
        got = (rank0 == j) & (mine > 0.5) & (iota((32, LANES), 1) < 12)
        table.append(jnp.sum(jnp.where(got, rows1, 0), axis=0, keepdims=True))
    table = jnp.concatenate(table, axis=0)
    table3 = jnp.zeros((RMAX, LANES), f32)
    last = jnp.zeros((8, LANES), f32)
    row8 = iota((8, LANES), 0)
    lane8 = iota((8, LANES), 1)
    for p in range(3):
        a, b, c = SHIFTS[p], SHIFTS[(p + 1) % 3], SHIFTS[(p + 2) % 3]
        ma, mb, mc = (me >> a) & 3, (me >> b) & 3, (me >> c) & 3

        def line_of(base):
            return jnp.concatenate(
                [present[pl.ds(pl.multiple_of(with_coord(base, a, s) * 32, 32), 32), :] for s in range(4)],
                axis=0,
            )

        here = line_of(me)
        rank1 = mm(strict_block, here)
        at1 = jnp.sum(jnp.where(lane == p * 4 + ma, rank1, 0.0), axis=1, keepdims=True)
        at1 = at1 + (((ma - (iota((LANES, 1), 0) >> 5)) & 3) * 64).astype(f32)
        rank2 = mm(strict, here)
        use = (here > 0.5) & (lane >> 4 == p + 1)
        rank2 = jnp.where(use, rank2, -1.0)
        extra = []
        for j in range(RMAX):
            extra.append(jnp.sum(jnp.where(rank2 == j, at1, 0.0), axis=0, keepdims=True))
        table = table + jnp.concatenate(extra, axis=0).astype(jnp.int32)

        found = [jnp.zeros((1, LANES), f32) for _ in range(4)]
        count = [jnp.zeros((1, LANES), f32) for _ in range(4)]
        for sb in range(4):
            base = with_coord(me, b, sb)
            there = line_of(base)
            order = mm(strict, there)
            at2 = jnp.sum(jnp.where(lane == 16 + p * 16 + ma * 4 + mb, order, 0.0), axis=1, keepdims=True)
            at2 = at2 + (((mb - sb) & 3) * 64).astype(f32)
            unit = iota((LANES, 1), 0)
            code = (base - (((base >> a) & 3) << a) + ((unit >> 5) << a)) * 32 + (unit & 31)
            for d in range(4):
                asks = g_ref[pl.ds(with_coord(me, c, d), 1), :]
                same = code == asks
                found[d] = found[d] + jnp.sum(jnp.where(same, at2, 0.0), axis=0, keepdims=True)
                count[d] = count[d] + jnp.sum(same.astype(f32), axis=0, keepdims=True)
        rank3 = mm(jnp.concatenate(count + count, axis=0), upper)
        lane32 = iota((RMAX, LANES), 1)
        for d in range(4):
            take = (rank3[d : d + 1] == iota((RMAX, LANES), 0).astype(f32)) & (count[d] > 0.5)
            column = jnp.sum(jnp.where(take, found[d], 0.0), axis=1, keepdims=True)
            table3 = table3 + jnp.where(lane32 == p * 4 + d, column, 0.0)
        asks = g_ref[pl.ds(me, 1), :]
        chosen = [((asks >= 0) & (((asks >> (5 + c)) & 3) == v)).astype(f32) for v in range(4)]
        spots = mm(jnp.concatenate(chosen + chosen, axis=0), upper)
        final = jnp.zeros((1, LANES), f32)
        for v in range(4):
            final = final + chosen[v] * (spots[v : v + 1] + (((mc - v) & 3) * 64).astype(f32))
        last = last + jnp.where(row8 == p, final, 0.0)
    last = last + jnp.where((row8 == 3) & (lane8 == 0), need1, 0.0)
    last = last + jnp.where((row8 == 3) & (lane8 == 1), need2, 0.0)
    last = last + jnp.where((row8 == 3) & (lane8 == 2), need3, 0.0)
    out_ref[0:32, :] = table
    out_ref[32:64, :] = table3.astype(jnp.int32)
    out_ref[64:72, :] = last.astype(jnp.int32)


def route(me, everyone):
    return pl.pallas_call(
        route_kernel,
        out_shape=jax.ShapeDtypeStruct((72, LANES), jnp.int32),
        in_specs=[pl.BlockSpec(memory_space=pltpu.SMEM), pl.BlockSpec(memory_space=pltpu.VMEM)],
        out_specs=pl.BlockSpec(memory_space=pltpu.VMEM),
        scratch_shapes=[pltpu.VMEM((2048, LANES), f32)],
    )(me, everyone)


def along(n, stride, step):
    here = (n // stride) % 4
    return n + ((here + step) % 4 - here) * stride


def gather_kernel(mine_ref, all_ref, send, recv, keep):
    n, m = lax.axis_index("db"), lax.axis_index("mp")
    z, y, x = n // 16, (n // 4) % 4, n % 4
    barrier = pltpu.get_barrier_semaphore()
    for stride in STRIDES:
        for step in (1, 2, 3):
            pl.semaphore_signal(
                barrier, inc=1, device_id={"db": along(n, stride, step), "mp": m}, device_id_type=MESH
            )
    pl.semaphore_wait(barrier, 9)
    own = pltpu.make_async_copy(mine_ref, all_ref.at[z, y, x], keep)
    own.start()
    own.wait()
    for axis, stride in enumerate(STRIDES):
        where = [(z, y, x), (slice(None), y, x), (slice(None), slice(None), x)][axis]
        copies = []
        for step in (1, 2, 3):
            copies.append(
                pltpu.make_async_remote_copy(
                    src_ref=all_ref.at[where],
                    dst_ref=all_ref.at[where],
                    send_sem=send.at[axis, step - 1],
                    recv_sem=recv.at[axis, step - 1],
                    device_id={"db": along(n, stride, step), "mp": m},
                    device_id_type=MESH,
                )
            )
        for copy in copies:
            copy.start()
        for copy in copies:
            copy.wait()


def gather_asks(mine):
    return pl.pallas_call(
        gather_kernel,
        out_shape=jax.ShapeDtypeStruct((4, 4, 4, 1, LANES), jnp.int32),
        in_specs=[pl.BlockSpec(memory_space=pltpu.VMEM)],
        out_specs=pl.BlockSpec(memory_space=pltpu.VMEM),
        scratch_shapes=[
            pltpu.SemaphoreType.DMA((3, 3)),
            pltpu.SemaphoreType.DMA((3, 3)),
            pltpu.SemaphoreType.DMA,
        ],
        compiler_params=pltpu.CompilerParams(collective_id=0, has_side_effects=True),
    )(mine)


def fetch_kernel(caps, table, database, fetched, *scratch):
    c1, c2, c3 = caps
    stores, stages, first, second, third = [scratch[3 * i : 3 * i + 3] for i in range(5)]
    whole, send, recv, load, local_sem, pair_send, pair_recv = scratch[15:]
    n, m = lax.axis_index("db"), lax.axis_index("mp")
    loads = []
    for p, (start, width) in enumerate(PARTS):
        loads.append(pltpu.make_async_copy(database.at[:, :, start : start + width], stores[p], load.at[p]))
        loads[p].start()
    coords = (n // 16, (n // 4) % 4, n % 4)
    barrier = pltpu.get_barrier_semaphore()
    for stride in STRIDES:
        for step in (1, 2, 3):
            pl.semaphore_signal(
                barrier, inc=1, device_id={"db": along(n, stride, step), "mp": m}, device_id_type=MESH
            )
    pl.semaphore_signal(barrier, inc=1, device_id={"db": n, "mp": 1 - m}, device_id_type=MESH)
    pl.semaphore_wait(barrier, 10)

    def blend(values, p):
        return values[p % 3] + m * (values[(p + 1) % 3] - values[p % 3])

    def turn(p):
        return (p + m) % 3

    def peer(p, hop, step):
        here = blend(coords, p + hop)
        return n + ((here + step) % 4 - here) * blend(STRIDES, p + hop)

    def copy_of(p, hop, step, count, landing):
        return pltpu.make_async_remote_copy(
            src_ref=stages[p].at[step - 1, pl.ds(0, count)],
            dst_ref=landing.at[step],
            send_sem=send.at[p, hop, step - 1],
            recv_sem=recv.at[p, hop, step - 1],
            device_id={"db": peer(p, hop, step), "mp": m},
            device_id_type=MESH,
        )

    def run_hop(p, hop, count, source, landing, row, lane_of):
        for step in (2, 1, 3, 0):
            lane = lane_of(step)
            into = landing.at[0] if step == 0 else stages[p].at[step - 1]

            def move(j, carry):
                code = table[row + j, lane]
                if hop == 0:
                    into[j] = source[code]
                else:
                    into[j] = source[code // 64, code % 64]
                return carry

            lax.fori_loop(0, count, move, 0)
            if step:
                copy_of(p, hop, step, count, landing).start()

    def finish(p, hop, count, landing):
        for step in (1, 3, 2):
            copy_of(p, hop, step, count, landing).wait()

    for p in range(3):
        loads[p].wait()
        ma = blend(coords, p)
        run_hop(p, 0, c1, stores[p], first[p], 0, lambda s: turn(p) * 4 + (ma + s) % 4)
    for p in range(3):
        finish(p, 0, c1, first[p])
        ma, mb = blend(coords, p), blend(coords, p + 1)
        run_hop(p, 1, c2, first[p], second[p], 0,
                lambda s: 16 + turn(p) * 16 + ma * 4 + (mb + s) % 4)
    for p in range(3):
        finish(p, 1, c2, second[p])
        mc = blend(coords, p + 2)
        run_hop(p, 2, c3, second[p], third[p], 32, lambda s: turn(p) * 4 + (mc + s) % 4)
    for p in range(3):
        finish(p, 2, c3, third[p])
    chunks = 4
    asks = whole.shape[0]
    size = asks // chunks
    base = (n % 4) * 32
    pending = []
    for chunk in range(chunks):
        def place(j, carry):
            k = chunk * size + j
            for p, (start, width) in enumerate(PARTS):
                code = table[64 + turn(p), base + k]
                whole[k, :, start : start + width] = third[p][code // 64, code % 64]
            return carry

        lax.fori_loop(0, size, place, 0)
        part = pl.ds(chunk * size, size)
        near = pltpu.make_async_copy(whole.at[part], fetched.at[m, part], local_sem.at[chunk])
        far = pltpu.make_async_remote_copy(
            src_ref=whole.at[part],
            dst_ref=fetched.at[m, part],
            send_sem=pair_send.at[chunk],
            recv_sem=pair_recv.at[chunk],
            device_id={"db": n, "mp": 1 - m},
            device_id_type=MESH,
        )
        near.start()
        far.start()
        pending += [near, far]
    for copy in pending:
        copy.wait()


def fetch(variant, asks, table, database):
    caps = VARIANTS[variant]
    half = database.shape[1]
    rows = database.shape[0]

    def per_part(*lead):
        return [pltpu.VMEM(lead + (half, width), jnp.bfloat16) for _, width in PARTS]

    return pl.pallas_call(
        functools.partial(fetch_kernel, caps),
        out_shape=jax.ShapeDtypeStruct((2, asks, half, E), jnp.bfloat16),
        in_specs=[pl.BlockSpec(memory_space=pltpu.SMEM), pl.BlockSpec(memory_space=pl.ANY)],
        out_specs=pl.BlockSpec(memory_space=pl.ANY),
        scratch_shapes=[
            *per_part(rows),
            *per_part(3, max(caps)),
            *per_part(4, caps[0]),
            *per_part(4, caps[1]),
            *per_part(4, caps[2]),
            pltpu.VMEM((asks, half, E), jnp.bfloat16),
            pltpu.SemaphoreType.DMA((3, 3, 3)),
            pltpu.SemaphoreType.DMA((3, 3, 3)),
            pltpu.SemaphoreType.DMA((3,)),
            pltpu.SemaphoreType.DMA((4,)),
            pltpu.SemaphoreType.DMA((4,)),
            pltpu.SemaphoreType.DMA((4,)),
        ],
        compiler_params=pltpu.CompilerParams(
            collective_id=1 + variant, has_side_effects=True, vmem_limit_bytes=63 * 2**20
        ),
    )(table, database)


def attend_kernel(rows_ref, query_ref, key_ref, value_ref, out_ref, keys, values):
    spans = rows_ref.shape[1] // 2
    half = rows_ref.shape[2]
    tokens = query_ref.shape[0] // spans
    rows = rows_ref[...].reshape(-1, E).astype(f32)
    mean = jnp.sum(rows * rows, axis=1, keepdims=True) * (1.0 / E)
    encoded = (rows * lax.rsqrt(mean + 1e-06)).astype(jnp.bfloat16)
    width = keys.shape[1]
    for start in range(0, width, 512):
        cut = slice(start, start + 512)
        keys[:, cut] = jnp.dot(encoded, key_ref[:, cut], preferred_element_type=f32).astype(jnp.bfloat16)
        values[:, cut] = jnp.dot(encoded, value_ref[:, cut], preferred_element_type=f32).astype(jnp.bfloat16)
    far = spans * 2 * half
    for span in range(spans):
        near = slice(span * 2 * half, (span + 1) * 2 * half)
        away = slice(far + span * 2 * half, far + (span + 1) * 2 * half)
        for head in range(width // HD):
            cut = slice(head * HD, (head + 1) * HD)
            key = jnp.concatenate([keys[near, cut], keys[away, cut]], axis=0)
            value = jnp.concatenate([values[near, cut], values[away, cut]], axis=0)
            query = query_ref[span * tokens : (span + 1) * tokens, cut]
            score = lax.dot_general(query, key, (((1,), (1,)), ((), ())), preferred_element_type=f32)
            score = score * (1.0 / math.sqrt(HD))
            power = jnp.exp(score - jnp.max(score, axis=1, keepdims=True))
            weight = (power / jnp.sum(power, axis=1, keepdims=True)).astype(jnp.bfloat16)
            mixed = jnp.dot(weight, value, preferred_element_type=f32)
            out_ref[span * tokens : (span + 1) * tokens, cut] = mixed.astype(jnp.bfloat16)


def attend(fetched, queries, w_key, w_value, span_total):
    spans = 2
    half = fetched.shape[2]
    width = w_key.shape[1]
    tokens = queries.shape[0] // span_total
    whole = pl.BlockSpec((E, width), lambda i: (0, 0), pipeline_mode=pl.Buffered(1))
    return pl.pallas_call(
        attend_kernel,
        grid=(span_total // spans,),
        out_shape=jax.ShapeDtypeStruct(queries.shape, jnp.bfloat16),
        in_specs=[
            pl.BlockSpec((2, 2 * spans, half, E), lambda i: (0, i, 0, 0)),
            pl.BlockSpec((spans * tokens, width), lambda i: (i, 0)),
            whole,
            whole,
        ],
        out_specs=pl.BlockSpec((spans * tokens, width), lambda i: (i, 0)),
        scratch_shapes=[pltpu.VMEM((4 * spans * half, width), jnp.bfloat16)] * 2,
        compiler_params=pltpu.CompilerParams(
            dimension_semantics=("arbitrary",), vmem_limit_bytes=60 * 2**20
        ),
    )(fetched, queries, w_key, w_value)


def body(queries, database, neighbour_shard, neighbour_row, w_key, w_value):
    span_total = neighbour_shard.shape[0]
    asks = span_total * neighbour_shard.shape[1]
    me = lax.axis_index("db")
    code = (neighbour_shard * 32 + neighbour_row).reshape(1, asks)
    code = jnp.pad(code, ((0, 0), (0, 32 - asks)), constant_values=-1)
    code = jnp.tile(code, (1, 4))
    code = jnp.where(jnp.arange(LANES)[None, :] // 32 == me % 4, code, -1)
    everyone = gather_asks(code).reshape(64, LANES)
    table = route(me.reshape(1), everyone)
    needs = table[67, :3]
    fits = jnp.array([jnp.all(needs <= jnp.array(caps)) for caps in VARIANTS[:-1]])
    choice = jnp.sum(jnp.cumprod(1 - fits.astype(jnp.int32)))
    branches = [functools.partial(fetch, v, asks) for v in range(len(VARIANTS))]
    fetched = lax.switch(choice, branches, table, database)
    return attend(fetched, queries, w_key, w_value, span_total)


def solution(mesh):
    placed = (
        P("db", "mp"),
        P("db", "mp", None),
        P("db", None),
        P("db", None),
        P(None, "mp"),
        P(None, "mp"),
    )
    return jax.shard_map(body, mesh=mesh, in_specs=placed, out_specs=P("db", "mp"), check_vma=False)
```

time: 675 us -> 262 us (0.39)
  waiting for transfers between devices: 469 us -> 0 us
  Pallas kernels: 0 us -> 252 us
  matrix products: 81.3 us -> 0 us
  local copies, waits for them, and re-layouts: 69.8 us -> 0.27 us
  other arithmetic: 23.8 us -> 5.45 us
  blocking collectives: 17 us -> 0 us
  starting transfers between devices: 9.36 us -> 0 us
    all_to_all x1 -> x0, waiting for transfers between devices: 469 us -> none  [body(): lax.all_to_all(doubled, ('db', 'mp'), split_axis=0, concat_axis=0, tiled=...]
    pallas_call x0 -> x4, Pallas kernels: none -> 252 us  [the longest x1 125 us: fetch(): pl.pallas_call(functools.partial(fetch_kernel, caps), out_shape=jax.Shape...]
    dot_general x4 -> x0, matrix products: 81.3 us -> none  [the longest x1 36 us: attend(): jnp.einsum('chmn,cnhd->cmhd', weights, value_rows, preferred_element_type...]
    unnamed x16 -> x0, local copies, waits for them, and re-layouts: 25.5 us -> none
    gather x2 -> x0, local copies, waits for them, and re-layouts: 24.4 us -> none  [the longest x1 13.4 us: body(): picked = arrived[shard_list, :, slot_list]]
    all_to_all x1 -> x0, blocking collectives: 17 us -> none  [body(): lax.all_to_all(wanted, 'db', split_axis=0, concat_axis=0, tiled=True)]
    broadcast_in_dim x1 -> x0, local copies, waits for them, and re-layouts: 14.2 us -> none  [body(): jnp.broadcast_to(outgoing[:, None], (shards, core_total, CAP, half_rows, E))]
    sub x1, other arithmetic: 15.1 us -> 1.97 us  [body(): choice = jnp.sum(jnp.cumprod(1 - fits.astype(jnp.int32)))]
  transfers between devices with their start and end apart: 1 -> 0, of which waited for: 1 -> 0; matrix products, arithmetic and copies ran while one was open for 1% -> 0% of each run, Pallas kernels for 0% -> 0%
where the time goes in v1:
time: 262 us; the launch traced here: 259 us
  Pallas kernels  252 us (96%)
  other arithmetic  5.45 us (2%)
    pallas_call x1, Pallas kernels, fetch(): pl.pallas_call(functools.partial(fetch_kernel, caps), out_shape=jax.Shape...  125 us
    pallas_call x1, Pallas kernels, attend(): pl.pallas_call(attend_kernel, grid=(span_total // spans,), out_shape=jax....  107 us
    pallas_call x1, Pallas kernels, gather_asks(): pl.pallas_call(gather_kernel, out_shape=jax.ShapeDtypeStruct((4, 4, 4, 1,...  15 us
    pallas_call x1, Pallas kernels, route(): pl.pallas_call(route_kernel, out_shape=jax.ShapeDtypeStruct((72, LANES),...  5.63 us

profile of v1, /device:TPU:28, one launch (start us, length us, event | category | flops | bytes accessed | tf_op | source)
XLA Modules:
  0.0 258.9 jit_solution(6120365340359226820)
XLA Ops:
  0.0 0.7 multiply_add_fusion
  0.7 0.1 copy.12
  0.8 0.1 reshape.144
  0.9 0.1 tile.13
  1.0 0.5 compare_select_fusion.mine_ref
  1.5 15.0 %shard_map.91 = s32[4,4,4,1,128]{4,3,2,1,0:T(1,128)} custom-call(s32[1,128]{1,0:T(1,128)} %compare_select_fusion.mine_ref), custom_call_target="tpu_custom_call" | custom-call | tf_op jit(solution)/shard_map/pallas_call | solution.py:204
  16.5 5.6 %shard_map.92 = s32[72,128]{1,0:T(8,128)S(1)} custom-call(s32[1]{0:T(128)} %bitcast.me_ref, s32[64,128]{1,0:T(8,128)} %bitcast.7), custom_call_target="tpu_custom_call" | custom-call | tf_op jit(solution)/shard_map/pallas_call | solution.py:156
  22.2 1.4 compare_reduce_fusion.2
  23.6 2.0 fusion
  25.6 0.2 reduce-window.6
  25.7 0.6 reduce_sum.9
  27.0 125.1 %conditional.1 = (bf16[2,28,64,896]{3,2,1,0:T(8,128)(2,1)}) conditional(s32[]{:T(128)} %clamp.3, (s32[72,128]{1,0:T(8,128)S(1)}, bf16[32,64,896]{2,1,0:T(8,128)(2,1)}) %tuple.17, (s32[72,128]{1,0:T(8,128)S(1)}, bf16[32,64,896]{2,1,0:T(8,128)(2,1)}) %tuple.17, (s32[72,128]{1,0:T(8,128)S(1)}, ...), branch_computations={%region_5.6_spmd, %region_6.7_spmd, %region_7.8_spmd, %region_8.9_... | conditional | bytes 8 | solution.py:424
  27.1 124.9 %branch_1_fun.1 = bf16[2,28,64,896]{3,2,1,0:T(8,128)(2,1)} custom-call(s32[72,128]{1,0:T(8,128)S(1)} %get-tuple-element.28.table, bf16[32,64,896]{2,1,0:T(8,128)(2,1)} %get-tuple-element.29.database), custom_call_target="tpu_custom_call" | custom-call | tf_op jit(solution)/shard_map/cond/branch_1_fun/pallas_call | solution.py:332
  152.2 106.8 %shard_map.93 = bf16[896,2048]{1,0:T(8,128)(2,1)} custom-call(bf16[2,28,64,896]{3,2,1,0:T(8,128)(2,1)} %get-tuple-element.37.rows_ref, bf16[896,2048]{1,0:T(8,128)(2,1)} %query_ref.1, bf16[896,2048]{1,0:T(8,128)(2,1)} %key_ref.1, bf16[896,2048]{1,0:T(8,128)(2,1)} %value_ref.1), custom_call_target="tpu_custom_call" | custom-call | tf_op jit(solution)/shard_map/pallas_call | solution.py:392
  (2 shorter events, 0.0 us)
